TPU v7x, 128 devices: a whole 4x4x4 slice. The times are simulated.
128 devices in a mesh: row: 8 (over y, core), col: 16 (over z, x).
Axes of the slice: x: 4, y: 4, z: 4, core: 2. Of those that a mesh axis runs over, the one named last changes fastest.
Arguments:
- wavefunction: bfloat16 [4096, 4096], P('row', 'col'), may hold values from -6 to 6
- left_env: bfloat16 [4, 4096, 4096], P(None, 'row'), may hold values from -0.09375 to 0.09375
- right_env: bfloat16 [4, 4096, 4096], P(None, None, 'col'), may hold values from -0.09375 to 0.09375
- filled_blocks: int32 [32, 32], replicated, may hold values 0 or 1
- term_columns: int32 [4, 32], replicated, may hold values 0 or 1
Outputs:
- product: bfloat16 [4096, 4096], P('row', 'col')
All inputs are finite; a program needn't handle non-finite values.
Results may differ from a plain program's by a relative error of at most 0.001.
Values may be sent and summed in bfloat16 or wider, within the bound.
A program may use at most 128 MiB of HBM per device.

v0:
```python
import jax
import jax.numpy as jnp
from jax import lax
from jax.sharding import PartitionSpec as P

BLOCK = 128


def on_device(wavefunction, left_env, right_env, filled_blocks, term_columns):
    row_count = wavefunction.shape[0]
    col_count = wavefunction.shape[1]
    row_blocks = row_count // BLOCK
    col_blocks = col_count // BLOCK
    row_place = lax.axis_index("row")
    col_place = lax.axis_index("col")
    filled_here = lax.dynamic_slice(
        filled_blocks, (row_place * row_blocks, col_place * col_blocks), (row_blocks, col_blocks)
    )
    block_gate = filled_here[:, None, :, None]
    masked_psi = (
        wavefunction.reshape(row_blocks, BLOCK, col_blocks, BLOCK) * block_gate.astype(jnp.bfloat16)
    ).reshape(row_count, col_count)
    column_gate = jnp.repeat(term_columns, BLOCK, axis=1).astype(jnp.bfloat16)
    acting = left_env * column_gate[:, None, :]
    window = right_env
    right_terms = jnp.einsum(
        "kc,tcb->tkb",
        lax.all_gather(masked_psi, "col", axis=1, tiled=True),
        window,
        preferred_element_type=jnp.float32,
    )
    window = acting.astype(jnp.float32)
    summed = jnp.einsum(
        "tak,tkb->ab",
        window,
        lax.all_gather(right_terms, "row", axis=1, tiled=True),
        precision=lax.Precision.HIGHEST,
        preferred_element_type=jnp.float32,
    )
    result = summed.reshape(row_blocks, BLOCK, col_blocks, BLOCK) * block_gate.astype(jnp.float32)
    return result.reshape(row_count, col_count).astype(jnp.bfloat16)


def solution(mesh):
    in_specs = (P("row", "col"), P(None, "row", None), P(None, None, "col"), P(), P())
    out_specs = P("row", "col")
    return jax.shard_map(
        on_device, mesh=mesh, in_specs=in_specs, out_specs=out_specs, check_vma=False
    )
```

profile of v0, /device:TPU:1, one launch (start us, length us, event | category | flops | bytes accessed | tf_op | source)
XLA Modules:
  0.0 192.3 jit_solution(575953007957870625)
XLA Ops:
  6.5 0.0 all-gather.3.cloned.1.call-start
  6.5 0.8 dynamic-slice_convert_fusion
  7.3 0.2 mul.40
  7.5 0.0 copy-start
  7.5 1.7 bitcast_multiply_fusion
  9.2 0.0 all-gather.3.cloned.1.call-update
  9.2 0.0 all-gather.5.cloned.1.call-start
  9.3 59.0 %all-gather.3.cloned.1.call-done = bf16[512,4096]{1,0:T(8,128)(2,1)} async-done(((bf16[512,256]{1,0:T(8,128)(2,1)}), bf16[512,4096]{1,0:T(8,128)(2,1)}) %all-gather.3.cloned.1.call-update) | async-done | bytes 4194320 | tf_op jit(solution)/shard_map/all_gather | solution.py:28
  68.3 10.5 %fusion.5 = f32[4,512,256]{2,1,0:T(8,128)} fusion(bf16[4,4096,256]{2,1,0:T(8,128)(2,1)} %param.7, bf16[512,4096]{1,0:T(8,128)(2,1)} %all-gather.3.cloned.1.call-done), kind=kOutput, calls=%fused_computation.5 | convolution fusion | flops 4294967296 | bytes 14680064 | tf_op jit(solution)/shard_map/kc,tcb->tkb/dot_general | solution.py:26
  78.8 0.0 all-gather.5.cloned.1.call-update
  78.8 0.0 copy-done
  78.8 0.1 broadcast_bitcast_fusion
  78.9 86.0 %all-gather.5.cloned.1.call-done = f32[4,4096,256]{2,1,0:T(8,128)} async-done(((f32[4,512,256]{2,1,0:T(8,128)}), f32[4,4096,256]{2,1,0:T(8,128)}) %all-gather.5.cloned.1.call-update) | async-done | bytes 16777232 | tf_op jit(solution)/shard_map/all_gather | solution.py:36
  164.9 0.2 mul.43
  165.1 20.3 %fusion.14 = bf16[512,256]{1,0:T(8,128)(2,1)} fusion(f32[4,4096,256]{2,1,0:T(8,128)} %all-gather.5.cloned.1.call-done, bf16[4,512,4096]{2,1,0:T(8,128)(2,1)} %param.6, bf16[4,4096]{1,0:T(4,128)(2,1)S(1)} %bitcast.30, f32[64,8,2,128]{3,2,1,0:T(2,128)S(1)} %bitcast.28), kind=kOutput, calls=%fused_computation.8 | convolution fusion | flops 25778454528 | bytes 34373632 | tf_op jit(solution)/shard_map/tak,tkb->ab/dot_general | solution.py:33
  (2 shorter events, 0.0 us)
Async XLA Ops:
  6.5 61.7 %all-gather.3.cloned.1.call-start = ((), (), s32[]{:S(2)}) async-start(), calls=%async_computation | async-start | bytes 4456448 | tf_op jit(solution)/shard_map/all_gather | solution.py:28
  7.5 71.3 %copy-start = (s32[4,32]{1,0:T(4,128)S(1)}, s32[4,32]{1,0:T(4,128)}, u32[]{:S(2)}) copy-start(s32[4,32]{1,0:T(4,128)} %param.9) | copy-start | bytes 1540
  9.2 155.6 %all-gather.5.cloned.1.call-start = ((), (), s32[]{:S(2)}) async-start(), calls=%async_computation.1 | async-start | bytes 18874368 | tf_op jit(solution)/shard_map/all_gather | solution.py:36
Sparse Core Ops, SparseCore 0:
  9.4 58.7 all-gather.2
  78.9 85.9 all-gather.4
where the time goes:
time: 192 us
  waiting for transfers between devices  145 us (76%)
  matrix products  30.8 us (16%)
  between operations  13.4 us (7%)
  other arithmetic  2.47 us (1%)
    all_gather x1, waiting for transfers between devices, on_device(): lax.all_gather(right_terms, 'row', axis=1, tiled=True)  86 us
    all_gather x1, waiting for transfers between devices, on_device(): lax.all_gather(masked_psi, 'col', axis=1, tiled=True)  59 us
    dot_general x1, matrix products, on_device(): jnp.einsum('tak,tkb->ab', window, lax.all_gather(right_terms, 'row', axis...  20.3 us
    dot_general x1, matrix products, on_device(): jnp.einsum('kc,tcb->tkb', lax.all_gather(masked_psi, 'col', axis=1, tiled...  10.5 us
  transfers between devices with their start and end apart: 2, of which 2 were waited for; matrix products, arithmetic and copies ran while one was open for 0% of the time, Pallas kernels for 0%

commit v1 on v0

v1 whole, which is shorter than its diff:
```python
import functools

import jax
import jax.numpy as jnp
from jax import lax
from jax.experimental import pallas as pl
from jax.experimental.pallas import tpu as pltpu
from jax.sharding import PartitionSpec as P

BLOCK = 128
TERMS = 4
BANDS = 4
HALF = BLOCK // 2
COLS = 256
CODED = TERMS * BLOCK + 16
TOP = 32766.0
MESH = pl.DeviceIdType.MESH


def kernel(psi, left, right, cmask, omask, gates, out, buf_a, buf_b, psim, right_v, left_v, zbuf, acc,
           s_a1, r_a1, s_a2, r_a2, s_b1, r_b1, s_b2, r_b2, loc, s_z, r_z, s_load):
    row = lax.axis_index("row")
    col = lax.axis_index("col")
    y, c = row // 2, row % 2
    z, x = col // 4, col % 4
    d = 1 - 2 * c
    xf, xb = (x + d + 4) % 4, (x - d + 4) % 4
    zf, zb = (z + d + 4) % 4, (z - d + 4) % 4
    yf, yb, y2 = (y + d + 4) % 4, (y - d + 4) % 4, (y + 2) % 4
    dev_xf, dev_xb = (row, z * 4 + xf), (row, z * 4 + xb)
    dev_zf, dev_zb = (row, zf * 4 + x), (row, zb * 4 + x)
    dev_yf, dev_yb = (yf * 2 + c, col), (yb * 2 + c, col)
    dev_sib = (y * 2 + 1 - c, col)

    def remote(src, dst, send, recv, dev):
        return pltpu.make_async_remote_copy(
            src_ref=src, dst_ref=dst, send_sem=send, recv_sem=recv, device_id=dev, device_id_type=MESH)

    loads = [pltpu.make_async_copy(right, right_v, s_load.at[0]), pltpu.make_async_copy(left, left_v, s_load.at[1])]
    for load in loads:
        load.start()

    barrier = pltpu.get_barrier_semaphore()
    for dev in (dev_xf, dev_xb, dev_zf, dev_zb, dev_yf, dev_yb, dev_sib):
        pl.semaphore_signal(barrier, inc=1, device_id=dev, device_id_type=MESH)
    pl.semaphore_wait(barrier, 7)

    def own_a(p):
        return psi.at[pl.ds(pl.multiple_of(p * BLOCK, BLOCK), HALF), :]

    def own_b(p):
        return psi.at[pl.ds(pl.multiple_of(p * BLOCK + HALF, HALF), HALF), :]

    def a1(p, slot):
        if slot == 2:
            return remote(buf_a.at[p, z, xb], buf_a.at[p, z, xb], s_a1.at[p, 2], r_a1.at[p, 2], dev_xf)
        return remote(own_a(p), buf_a.at[p, z, x], s_a1.at[p, slot], r_a1.at[p, slot], (dev_xf, dev_xb)[slot])

    def b1(p, slot):
        if slot == 2:
            return remote(buf_b.at[p, x, zb], buf_b.at[p, x, zb], s_b1.at[p, 2], r_b1.at[p, 2], dev_zf)
        return remote(own_b(p), buf_b.at[p, x, z], s_b1.at[p, slot], r_b1.at[p, slot], (dev_zf, dev_zb)[slot])

    def a2(p, slot):
        src = buf_a.at[p, zb] if slot == 2 else buf_a.at[p, z]
        return remote(src, src, s_a2.at[p, slot], r_a2.at[p, slot], (dev_zf, dev_zb, dev_zf)[slot])

    def b2(p, slot):
        src = buf_b.at[p, xb] if slot == 2 else buf_b.at[p, x]
        return remote(src, src, s_b2.at[p, slot], r_b2.at[p, slot], (dev_xf, dev_xb, dev_xf)[slot])

    def local_a(p):
        return pltpu.make_async_copy(own_a(p), buf_a.at[p, z, x], loc.at[p, 0])

    def local_b(p):
        return pltpu.make_async_copy(own_b(p), buf_b.at[p, x, z], loc.at[p, 1])

    def first_send(p):
        for slot in (0, 1):
            a1(p, slot).start()
            b1(p, slot).start()
        local_a(p).start()
        local_b(p).start()

    def first_forward(p):
        a1(p, 0).wait_recv()
        a1(p, 2).start()
        b1(p, 0).wait_recv()
        b1(p, 2).start()

    def second_send(p):
        local_a(p).wait()
        local_b(p).wait()
        a1(p, 1).wait_recv()
        b1(p, 1).wait_recv()
        a1(p, 2).wait_recv()
        for slot in (0, 1):
            a2(p, slot).start()
        b1(p, 2).wait_recv()
        for slot in (0, 1):
            b2(p, slot).start()

    def second_forward(p):
        a2(p, 0).wait_recv()
        a2(p, 2).start()
        b2(p, 0).wait_recv()
        b2(p, 2).start()

    def second_wait(p):
        for slot in (1, 2):
            a2(p, slot).wait_recv()
            b2(p, slot).wait_recv()

    def z_copy(p, which):
        block = zbuf.at[(row, row, row, yb * 2 + c, yb * 2 + c, yf * 2 + c, y2 * 2 + c)[which], p]
        arrives = (2, 3, 1, 6, 4, 5, 7)[which]
        dev = (dev_yf, dev_yb, dev_sib, dev_yf, dev_sib, dev_sib, dev_sib)[which]
        return remote(block, block, s_z.at[p, which], r_z.at[p, arrives], dev)

    eye = lax.broadcasted_iota(jnp.int32, (BLOCK, BLOCK), 0) == lax.broadcasted_iota(jnp.int32, (BLOCK, BLOCK), 1)
    lines = lax.broadcasted_iota(jnp.int32, (16, BLOCK), 0)

    def make_z(p):
        for j in range(16):
            gate = cmask[p, :, j * COLS:(j + 1) * COLS]
            psim[:HALF, j * COLS:(j + 1) * COLS] = buf_a[p, j // 4, j % 4] * gate
            psim[HALF:, j * COLS:(j + 1) * COLS] = buf_b[p, j % 4, j // 4] * gate

        def term(t, scales):
            value = jnp.dot(psim[...], right_v[t], preferred_element_type=jnp.float32)
            top = jnp.maximum(jnp.max(jnp.abs(value), axis=1, keepdims=True), 1e-30)
            level = jnp.ceil(jnp.log2(top) * 256.0 + 0.05)
            code = jnp.round(value * (jnp.exp2(level * (-1.0 / 256.0)) * TOP))
            zbuf[row, p, pl.ds(pl.multiple_of(t * BLOCK, BLOCK), BLOCK), :] = code.astype(jnp.int32).astype(jnp.int16)
            line = jnp.sum(jnp.where(eye, level, 0.0), axis=0, keepdims=True)
            return jnp.where(lines == t, line, scales)

        scales = lax.fori_loop(0, TERMS, term, jnp.zeros((16, BLOCK), jnp.float32))
        zbuf[row, p, TERMS * BLOCK:, :BLOCK] = scales.astype(jnp.int32).astype(jnp.int16)
        zbuf[row, p, TERMS * BLOCK:, BLOCK:] = jnp.zeros((16, BLOCK), jnp.int16)

    def use_z(src, p):
        band = src * BANDS + p
        levels = zbuf[src, p, TERMS * BLOCK:, :BLOCK].astype(jnp.int32).astype(jnp.float32)
        high, low, factors = [], [], []
        for t in range(TERMS):
            scale = jnp.exp2(levels[t:t + 1, :] * (1.0 / 256.0)) * (gates[t, band].astype(jnp.float32) / TOP)
            scale = jnp.sum(jnp.where(eye, scale, 0.0), axis=1, keepdims=True)
            value = zbuf[src, p, t * BLOCK:(t + 1) * BLOCK, :].astype(jnp.int32).astype(jnp.float32) * scale
            top = value.astype(jnp.bfloat16)
            high.append(top)
            low.append((value - top.astype(jnp.float32)).astype(jnp.bfloat16))
            factors.append(left_v[t, :, pl.ds(pl.multiple_of(band * BLOCK, BLOCK), BLOCK)])
        acc[...] += jnp.dot(jnp.concatenate(factors + factors, axis=1), jnp.concatenate(high + low, axis=0),
                            preferred_element_type=jnp.float32)

    acc[...] = jnp.zeros_like(acc)
    first_send(0)
    first_send(1)
    first_forward(0)
    second_send(0)
    first_send(2)
    first_forward(1)
    second_send(1)
    first_send(3)
    loads[0].wait()

    def step(s, carry):
        @pl.when(s < BANDS)
        def _():
            second_forward(s)
            second_wait(s)
            make_z(s)
            for which in range(3):
                z_copy(s, which).start()

        @pl.when(s < BANDS - 2)
        def _():
            first_forward(s + 2)
            second_send(s + 2)

        @pl.when(s == 1)
        def _():
            loads[1].wait()

        def arrival(r, carry):
            late = jnp.where(r >= 7, 3, jnp.where(r >= 4, 2, 1))
            p = s - late

            @pl.when((p >= 0) & (p < BANDS))
            def _():
                @pl.when(r > 0)
                def _():
                    block = zbuf.at[0, 0]
                    remote(block, block, s_z.at[p, 0], r_z.at[p, r], dev_sib).wait_recv()

                @pl.when(r == 2)
                def _():
                    z_copy(p, 3).start()
                    z_copy(p, 4).start()

                @pl.when(r == 3)
                def _():
                    z_copy(p, 5).start()

                @pl.when(r == 6)
                def _():
                    z_copy(p, 6).start()

                y_of = jnp.where(r < 2, y, jnp.where(r >= 6, y2, jnp.where((r == 2) | (r == 5), yb, yf)))
                other = jnp.where((r == 1) | (r == 4) | (r == 5) | (r == 7), 1, 0)
                core = c + other * d
                use_z(y_of * 2 + core, p)

            return carry

        return lax.fori_loop(0, 8, arrival, carry)

    lax.fori_loop(0, BANDS + 3, step, 0)

    for i in range(4):
        out[i * BLOCK:(i + 1) * BLOCK, :] = (acc[i * BLOCK:(i + 1) * BLOCK, :] * omask[i]).astype(jnp.bfloat16)

    def drain(p, carry):
        for slot in range(3):
            for copy in (a1, b1, a2, b2):
                copy(p, slot).wait_send()
        for which in range(7):
            z_copy(p, which).wait_send()
        return carry

    lax.fori_loop(0, BANDS, drain, 0)


def on_device(wavefunction, left_env, right_env, filled_blocks, term_columns):
    row_place = lax.axis_index("row")
    col_place = lax.axis_index("col")
    filled_rows = lax.dynamic_slice(filled_blocks, (row_place * BANDS, 0), (BANDS, filled_blocks.shape[1]))
    cmask = jnp.repeat(filled_rows, BLOCK, axis=1).astype(jnp.bfloat16)[:, None, :]
    filled_here = lax.dynamic_slice(filled_rows, (0, col_place * 2), (BANDS, 2))
    omask = jnp.repeat(filled_here, BLOCK, axis=1).astype(jnp.float32)[:, None, :]
    any_space = pl.BlockSpec(memory_space=pl.ANY)
    vmem = pl.BlockSpec(memory_space=pltpu.VMEM)
    dma = pltpu.SemaphoreType.DMA
    return pl.pallas_call(
        kernel,
        out_shape=jax.ShapeDtypeStruct(wavefunction.shape, jnp.bfloat16),
        in_specs=[any_space, any_space, any_space, vmem, vmem, pl.BlockSpec(memory_space=pltpu.SMEM)],
        out_specs=vmem,
        scratch_shapes=[
            pltpu.VMEM((BANDS, 4, 4, HALF, COLS), jnp.bfloat16),
            pltpu.VMEM((BANDS, 4, 4, HALF, COLS), jnp.bfloat16),
            pltpu.VMEM((BLOCK, 4096), jnp.bfloat16),
            pltpu.VMEM((TERMS, 4096, COLS), jnp.bfloat16),
            pltpu.VMEM((TERMS, 512, 4096), jnp.bfloat16),
            pltpu.VMEM((8, BANDS, CODED, COLS), jnp.int16),
            pltpu.VMEM((512, COLS), jnp.float32),
        ] + [dma((BANDS, 3))] * 8 + [dma((BANDS, 2)), dma((BANDS, 7)), dma((BANDS, 8)), dma((2,))],
        compiler_params=pltpu.CompilerParams(
            collective_id=0, has_side_effects=True, vmem_limit_bytes=60 * 1024 * 1024),
    )(wavefunction, left_env, right_env, cmask, omask, term_columns)


def solution(mesh):
    in_specs = (P("row", "col"), P(None, "row", None), P(None, None, "col"), P(), P())
    return jax.shard_map(on_device, mesh=mesh, in_specs=in_specs, out_specs=P("row", "col"), check_vma=False)
```

time: 192 us -> 85.5 us (0.45)
  waiting for transfers between devices: 145 us -> 0 us
  Pallas kernels: 0 us -> 80.7 us
  matrix products: 30.8 us -> 0 us
  between operations: 13.4 us -> 0.02 us
  local copies, waits for them, and re-layouts: 0.51 us -> 3.06 us
    all_gather x2 -> x0, waiting for transfers between devices: 145 us -> none  [the longest x1 86 us: on_device(): lax.all_gather(right_terms, 'row', axis=1, tiled=True)]
    pallas_call x0 -> x1, Pallas kernels: none -> 80.7 us  [on_device(): pl.pallas_call(kernel, out_shape=jax.ShapeDtypeStruct(wavefunction.shape,...]
    dot_general x2 -> x0, matrix products: 30.8 us -> none  [the longest x1 20.3 us: on_device(): jnp.einsum('tak,tkb->ab', window, lax.all_gather(right_terms, 'row', axis...]
  transfers between devices with their start and end apart: 2 -> 0, of which waited for: 2 -> 0; matrix products, arithmetic and copies ran while one was open for 0% -> 0% of each run, Pallas kernels for 0% -> 0%
where the time goes in v1:
time: 85.5 us; the launch traced here: 85.3 us
  Pallas kernels  80.7 us (94%)
  local copies, waits for them, and re-layouts  3.06 us (4%)
  other arithmetic  1.46 us (2%)
    pallas_call x1, Pallas kernels, on_device(): pl.pallas_call(kernel, out_shape=jax.ShapeDtypeStruct(wavefunction.shape,...  80.7 us

profile of v1, /device:TPU:1, one launch (start us, length us, event | category | flops | bytes accessed | tf_op | source)
XLA Modules:
  0.0 85.3 jit_solution(5416134218507962537)
XLA Ops:
  0.0 0.7 dynamic-slice_convert_fusion.1
  0.7 0.8 dynamic-slice_convert_fusion
  1.5 0.7 broadcast_in_dim.9
  2.1 0.1 broadcast_in_dim.8
  2.2 0.6 convert_element_type.32.cmask
  2.9 80.7 %shard_map.55 = bf16[512,256]{1,0:T(8,128)(2,1)} custom-call(bf16[512,256]{1,0:T(8,128)(2,1)} %psi.1, bf16[4,512,4096]{2,1,0:T(8,128)(2,1)} %left.1, bf16[4,4096,256]{2,1,0:T(8,128)(2,1)} %right.1, bf16[4,1,4096]{2,1,0:T(2,128)(2,1)} %convert_element_type.32.cmask, f32[4,1,256]{2,1,0:T(1,128)} %bitcast.1, s32[4,32]{1,0:T(4,128)} %gates.1), custom_call_target="tpu_custom_call" | custom-call | tf_op jit(solution)/shard_map/pallas_call | solution.py:245
  83.6 1.7 %copy.8 = bf16[512,256]{1,0:T(8,128)(2,1)} copy(bf16[512,256]{1,0:T(8,128)(2,1)} %shard_map.55) | data formatting | bytes 524288

commit v2 on v1

--- a/solution.py
+++ b/solution.py
@@ -17,7 +17,7 @@
 MESH = pl.DeviceIdType.MESH
 
 
-def kernel(psi, left, right, cmask, omask, gates, out, buf_a, buf_b, psim, right_v, left_v, zbuf, acc,
+def kernel(psi, left, right, filled, gates, out, buf_a, buf_b, psim, right_v, left_v, zbuf, acc,
            s_a1, r_a1, s_a2, r_a2, s_b1, r_b1, s_b2, r_b2, loc, s_z, r_z, s_load):
     row = lax.axis_index("row")
     col = lax.axis_index("col")
@@ -37,29 +37,24 @@
             src_ref=src, dst_ref=dst, send_sem=send, recv_sem=recv, device_id=dev, device_id_type=MESH)
 
     loads = [pltpu.make_async_copy(right, right_v, s_load.at[0]), pltpu.make_async_copy(left, left_v, s_load.at[1])]
-    for load in loads:
-        load.start()
+    for p in range(BANDS):
+        pltpu.make_async_copy(psi.at[pl.ds(p * BLOCK, HALF), :], buf_a.at[p, z, x], loc.at[p, 0]).start()
+        pltpu.make_async_copy(psi.at[pl.ds(p * BLOCK + HALF, HALF), :], buf_b.at[p, x, z], loc.at[p, 1]).start()
 
     barrier = pltpu.get_barrier_semaphore()
     for dev in (dev_xf, dev_xb, dev_zf, dev_zb, dev_yf, dev_yb, dev_sib):
         pl.semaphore_signal(barrier, inc=1, device_id=dev, device_id_type=MESH)
     pl.semaphore_wait(barrier, 7)
 
-    def own_a(p):
-        return psi.at[pl.ds(pl.multiple_of(p * BLOCK, BLOCK), HALF), :]
-
-    def own_b(p):
-        return psi.at[pl.ds(pl.multiple_of(p * BLOCK + HALF, HALF), HALF), :]
-
     def a1(p, slot):
         if slot == 2:
             return remote(buf_a.at[p, z, xb], buf_a.at[p, z, xb], s_a1.at[p, 2], r_a1.at[p, 2], dev_xf)
-        return remote(own_a(p), buf_a.at[p, z, x], s_a1.at[p, slot], r_a1.at[p, slot], (dev_xf, dev_xb)[slot])
+        return remote(buf_a.at[p, z, x], buf_a.at[p, z, x], s_a1.at[p, slot], r_a1.at[p, slot], (dev_xf, dev_xb)[slot])
 
     def b1(p, slot):
         if slot == 2:
             return remote(buf_b.at[p, x, zb], buf_b.at[p, x, zb], s_b1.at[p, 2], r_b1.at[p, 2], dev_zf)
-        return remote(own_b(p), buf_b.at[p, x, z], s_b1.at[p, slot], r_b1.at[p, slot], (dev_zf, dev_zb)[slot])
+        return remote(buf_b.at[p, x, z], buf_b.at[p, x, z], s_b1.at[p, slot], r_b1.at[p, slot], (dev_zf, dev_zb)[slot])
 
     def a2(p, slot):
         src = buf_a.at[p, zb] if slot == 2 else buf_a.at[p, z]
@@ -69,18 +64,13 @@
         src = buf_b.at[p, xb] if slot == 2 else buf_b.at[p, x]
         return remote(src, src, s_b2.at[p, slot], r_b2.at[p, slot], (dev_xf, dev_xb, dev_xf)[slot])
 
-    def local_a(p):
-        return pltpu.make_async_copy(own_a(p), buf_a.at[p, z, x], loc.at[p, 0])
-
-    def local_b(p):
-        return pltpu.make_async_copy(own_b(p), buf_b.at[p, x, z], loc.at[p, 1])
-
     def first_send(p):
+        own_a, own_b = psi.at[pl.ds(0, HALF), :], psi.at[pl.ds(HALF, HALF), :]
+        pltpu.make_async_copy(own_a, buf_a.at[p, z, x], loc.at[p, 0]).wait()
+        pltpu.make_async_copy(own_b, buf_b.at[p, x, z], loc.at[p, 1]).wait()
         for slot in (0, 1):
             a1(p, slot).start()
             b1(p, slot).start()
-        local_a(p).start()
-        local_b(p).start()
 
     def first_forward(p):
         a1(p, 0).wait_recv()
@@ -89,8 +79,6 @@
         b1(p, 2).start()
 
     def second_send(p):
-        local_a(p).wait()
-        local_b(p).wait()
         a1(p, 1).wait_recv()
         b1(p, 1).wait_recv()
         a1(p, 2).wait_recv()
@@ -122,7 +110,9 @@
 
     def make_z(p):
         for j in range(16):
-            gate = cmask[p, :, j * COLS:(j + 1) * COLS]
+            gate = jnp.concatenate([
+                jnp.full((1, BLOCK), filled[row * BANDS + p, 2 * j + h].astype(jnp.float32)).astype(jnp.bfloat16)
+                for h in range(2)], axis=1)
             psim[:HALF, j * COLS:(j + 1) * COLS] = buf_a[p, j // 4, j % 4] * gate
             psim[HALF:, j * COLS:(j + 1) * COLS] = buf_b[p, j % 4, j // 4] * gate
 
@@ -154,37 +144,48 @@
         acc[...] += jnp.dot(jnp.concatenate(factors + factors, axis=1), jnp.concatenate(high + low, axis=0),
                             preferred_element_type=jnp.float32)
 
-    acc[...] = jnp.zeros_like(acc)
     first_send(0)
     first_send(1)
+    loads[0].start()
+    loads[1].start()
+    acc[...] = jnp.zeros_like(acc)
     first_forward(0)
     second_send(0)
+    first_forward(1)
     first_send(2)
-    first_forward(1)
+    first_send(3)
+    second_forward(0)
     second_send(1)
-    first_send(3)
+    first_forward(2)
     loads[0].wait()
 
     def step(s, carry):
         @pl.when(s < BANDS)
         def _():
-            second_forward(s)
             second_wait(s)
             make_z(s)
             for which in range(3):
                 z_copy(s, which).start()
 
+        @pl.when(s == 0)
+        def _():
+            loads[1].wait()
+
+        @pl.when(s < BANDS - 1)
+        def _():
+            second_forward(s + 1)
+
         @pl.when(s < BANDS - 2)
         def _():
-            first_forward(s + 2)
             second_send(s + 2)
 
-        @pl.when(s == 1)
-        def _():
-            loads[1].wait()
-
-        def arrival(r, carry):
-            late = jnp.where(r >= 7, 3, jnp.where(r >= 4, 2, 1))
+        @pl.when(s < BANDS - 3)
+        def _():
+            first_forward(s + 3)
+
+        def arrival(i, carry):
+            r = jnp.where(i == 3, 1, jnp.where((i == 1) | (i == 2), i + 1, i))
+            late = jnp.where((i == 0) | (i == 3), 0, jnp.where(i >= 6, 2, 1))
             p = s - late
 
             @pl.when((p >= 0) & (p < BANDS))
@@ -216,10 +217,13 @@
 
         return lax.fori_loop(0, 8, arrival, carry)
 
-    lax.fori_loop(0, BANDS + 3, step, 0)
+    lax.fori_loop(0, BANDS + 2, step, 0)
 
     for i in range(4):
-        out[i * BLOCK:(i + 1) * BLOCK, :] = (acc[i * BLOCK:(i + 1) * BLOCK, :] * omask[i]).astype(jnp.bfloat16)
+        for h in range(2):
+            keep = filled[row * BANDS + i, col * 2 + h].astype(jnp.float32)
+            where = (slice(i * BLOCK, (i + 1) * BLOCK), slice(h * BLOCK, (h + 1) * BLOCK))
+            out[where] = (acc[where] * keep).astype(jnp.bfloat16)
 
     def drain(p, carry):
         for slot in range(3):
@@ -233,19 +237,14 @@
 
 
 def on_device(wavefunction, left_env, right_env, filled_blocks, term_columns):
-    row_place = lax.axis_index("row")
-    col_place = lax.axis_index("col")
-    filled_rows = lax.dynamic_slice(filled_blocks, (row_place * BANDS, 0), (BANDS, filled_blocks.shape[1]))
-    cmask = jnp.repeat(filled_rows, BLOCK, axis=1).astype(jnp.bfloat16)[:, None, :]
-    filled_here = lax.dynamic_slice(filled_rows, (0, col_place * 2), (BANDS, 2))
-    omask = jnp.repeat(filled_here, BLOCK, axis=1).astype(jnp.float32)[:, None, :]
     any_space = pl.BlockSpec(memory_space=pl.ANY)
     vmem = pl.BlockSpec(memory_space=pltpu.VMEM)
+    smem = pl.BlockSpec(memory_space=pltpu.SMEM)
     dma = pltpu.SemaphoreType.DMA
     return pl.pallas_call(
         kernel,
         out_shape=jax.ShapeDtypeStruct(wavefunction.shape, jnp.bfloat16),
-        in_specs=[any_space, any_space, any_space, vmem, vmem, pl.BlockSpec(memory_space=pltpu.SMEM)],
+        in_specs=[any_space, any_space, any_space, smem, smem],
         out_specs=vmem,
         scratch_shapes=[
             pltpu.VMEM((BANDS, 4, 4, HALF, COLS), jnp.bfloat16),
@@ -258,7 +257,7 @@
         ] + [dma((BANDS, 3))] * 8 + [dma((BANDS, 2)), dma((BANDS, 7)), dma((BANDS, 8)), dma((2,))],
         compiler_params=pltpu.CompilerParams(
             collective_id=0, has_side_effects=True, vmem_limit_bytes=60 * 1024 * 1024),
-    )(wavefunction, left_env, right_env, cmask, omask, term_columns)
+    )(wavefunction, left_env, right_env, filled_blocks, term_columns)
 
 
 def solution(mesh):

time: 85.5 us -> 69.2 us (0.81)
  Pallas kernels: 80.7 us -> 67.3 us
  other arithmetic: 1.46 us -> 0 us
  local copies, waits for them, and re-layouts: 3.06 us -> 1.67 us
    pallas_call x1, Pallas kernels: 80.7 us -> 67.3 us  [on_device(): pl.pallas_call(kernel, out_shape=jax.ShapeDtypeStruct(wavefunction.shape,...]
    convert_element_type x2 -> x0, other arithmetic: 1.46 us -> none  [the longest x1 0.77 us: on_device(): jnp.repeat(filled_here, BLOCK, axis=1).astype(jnp.float32)[:, None, :]]
where the time goes in v2:
time: 69.2 us; the launch traced here: 68.9 us
  Pallas kernels  67.3 us (97%)
  local copies, waits for them, and re-layouts  1.67 us (2%)
    pallas_call x1, Pallas kernels, on_device(): pl.pallas_call(kernel, out_shape=jax.ShapeDtypeStruct(wavefunction.shape,...  67.3 us
    unnamed x1, local copies, waits for them, and re-layouts  1.67 us

profile of v2, /device:TPU:1, one launch (start us, length us, event | category | flops | bytes accessed | tf_op | source)
XLA Modules:
  0.0 68.9 jit_solution(9242280264496253239)
XLA Ops:
  0.0 67.3 %shard_map.55 = bf16[512,256]{1,0:T(8,128)(2,1)} custom-call(bf16[512,256]{1,0:T(8,128)(2,1)} %psi.1, bf16[4,512,4096]{2,1,0:T(8,128)(2,1)} %left.1, bf16[4,4096,256]{2,1,0:T(8,128)(2,1)} %right.1, s32[32,32]{1,0:T(8,128)} %filled.1, s32[4,32]{1,0:T(4,128)} %gates.1), custom_call_target="tpu_custom_call" | custom-call | tf_op jit(solution)/shard_map/pallas_call | solution.py:244
  67.3 1.7 %copy.7 = bf16[512,256]{1,0:T(8,128)(2,1)} copy(bf16[512,256]{1,0:T(8,128)(2,1)} %shard_map.55) | data formatting | bytes 524288

commit v3 on v0

v3 whole, which is shorter than its diff:
```python
import functools

import jax
import jax.numpy as jnp
from jax import lax
from jax.experimental import pallas as pl
from jax.experimental.pallas import tpu as pltpu
from jax.sharding import PartitionSpec as P

BLOCK = 128
TERMS = 4
COLS = 256
DEEP = 4096
TOP = 32766.0
MESH = pl.DeviceIdType.MESH
OWN = ((0, 64), (64, 64), (128, 128), (256, 128), (384, 128))
FAR = (4,)
GATHERS = [rows for _, rows in OWN] + [OWN[i][1] for i in FAR]
FAR_OF = {i: len(OWN) + f for f, i in enumerate(FAR)}
ORDER = (
    ("make", 0), ("make", 1), ("use", 0, 0), ("make", 2), ("take", 0, 2), ("take", 0, 3), ("use", 0, 1),
    ("use", 1, 0), ("take", 1, 2), ("take", 1, 3), ("use", 0, 2), ("use", 0, 3), ("use", 1, 1), ("make", 3),
    ("use", 0, 4), ("use", 0, 5), ("use", 2, 0), ("use", 2, 1), ("take", 2, 2), ("take", 2, 3), ("use", 1, 2),
    ("make", 4), ("take", 0, 6), ("take", 1, 6), ("use", 1, 3), ("use", 0, 6), ("use", 3, 0), ("use", 1, 4),
    ("use", 1, 5), ("use", 0, 7), ("make", 5), ("take", 3, 2), ("take", 3, 3), ("use", 3, 1), ("use", 2, 2),
    ("use", 2, 3), ("take", 2, 6), ("use", 3, 6), ("use", 1, 6), ("use", 2, 4), ("use", 2, 5), ("use", 3, 7),
    ("use", 1, 7), ("take", 4, 2), ("take", 4, 3), ("use", 3, 2), ("use", 3, 3), ("take", 3, 6), ("use", 2, 6),
    ("use", 3, 4), ("use", 3, 5), ("use", 2, 7),
)


def kernel(psi, left, right, filled, gates, out, *scratch):
    count = len(GATHERS)
    bufs_a, bufs_b = scratch[:count], scratch[count:2 * count]
    psim, right_v, left_v, z_small, z_large, acc, s_g, r_g, s_0, r_0, loc, s_z, r_z, s_load = scratch[2 * count:]
    row = lax.axis_index("row")
    col = lax.axis_index("col")
    y, c = row // 2, row % 2
    z, x = col // 4, col % 4
    d = 1 - 2 * c
    xf, xb, x2 = (x + d + 4) % 4, (x - d + 4) % 4, (x + 2) % 4
    zf, zb, z2 = (z + d + 4) % 4, (z - d + 4) % 4, (z + 2) % 4
    yf, yb, y2 = (y + d + 4) % 4, (y - d + 4) % 4, (y + 2) % 4
    dev_x = [(row, z * 4 + v) for v in (xf, xb, x2)]
    dev_z = [(row, v * 4 + x) for v in (zf, zb, z2)]
    dev_y = [(v * 2 + c, col) for v in (yf, yb, y2)]
    dev_sib = (y * 2 + 1 - c, col)

    def remote(src, dst, send, recv, dev):
        return pltpu.make_async_remote_copy(
            src_ref=src, dst_ref=dst, send_sem=send, recv_sem=recv, device_id=dev, device_id_type=MESH)

    loads = [pltpu.make_async_copy(right, right_v, s_load.at[0]), pltpu.make_async_copy(left, left_v, s_load.at[1])]

    def local(g):
        first, rows = OWN[g]
        half = rows // 2
        return (pltpu.make_async_copy(psi.at[pl.ds(first, half), :], bufs_a[g].at[z, x], loc.at[g, 0]),
                pltpu.make_async_copy(psi.at[pl.ds(first + half, half), :], bufs_b[g].at[x, z], loc.at[g, 1]))

    for g in range(len(OWN)):
        for copy in local(g):
            copy.start()

    barrier = pltpu.get_barrier_semaphore()
    partners = dev_x + dev_z + dev_y + [dev_sib]
    for dev in partners:
        pl.semaphore_signal(barrier, inc=1, device_id=dev, device_id_type=MESH)
    pl.semaphore_wait(barrier, len(partners))

    def one(g, slot):
        a, b = bufs_a[g].at[z, x], bufs_b[g].at[x, z]
        return (remote(a, a, s_g.at[g, slot], r_g.at[g, slot], dev_x[slot]),
                remote(b, b, s_g.at[g, 3 + slot], r_g.at[g, 3 + slot], dev_z[slot]))

    def two(g, slot):
        a, b = bufs_a[g].at[z], bufs_b[g].at[x]
        return (remote(a, a, s_g.at[g, 6 + slot], r_g.at[g, 6 + slot], dev_z[slot]),
                remote(b, b, s_g.at[g, 9 + slot], r_g.at[g, 9 + slot], dev_x[slot]))

    def far(f):
        i = FAR[f]
        g = FAR_OF[i]
        return (remote(bufs_a[i].at[z, x], bufs_a[g].at[z, x], s_0.at[f, 0], r_0.at[f, 0], dev_y[2]),
                remote(bufs_b[i].at[x, z], bufs_b[g].at[x, z], s_0.at[f, 1], r_0.at[f, 1], dev_y[2]))

    def send_one(g):
        if g >= len(OWN):
            for copy in far(g - len(OWN)):
                copy.wait_recv()
        for slot in range(3):
            for copy in one(g, slot):
                copy.start()

    def send_two(g):
        for slot in range(3):
            for copy in one(g, slot):
                copy.wait_recv()
        for slot in range(3):
            for copy in two(g, slot):
                copy.start()

    def wait_two(g):
        for slot in range(3):
            for copy in two(g, slot):
                copy.wait_recv()

    def coded(src, i):
        return z_small.at[src, i] if i < 2 else z_large.at[src, i - 2]

    def z_copy(i, which):
        block = coded((row, row, row, yb * 2 + c, yb * 2 + c, yf * 2 + c, y2 * 2 + c)[which], i)
        arrives = (2, 3, 1, 6, 4, 5, 7)[which]
        dev = (dev_y[0], dev_y[1], dev_sib, dev_y[0], dev_sib, dev_sib, dev_sib)[which]
        return remote(block, block, s_z.at[i, which], r_z.at[i, arrives], dev)

    def z_wait(i, r):
        block = coded(0, i)
        remote(block, block, s_z.at[i, 0], r_z.at[i, r], dev_sib).wait_recv()

    eye = lax.broadcasted_iota(jnp.int32, (BLOCK, BLOCK), 0) == lax.broadcasted_iota(jnp.int32, (BLOCK, BLOCK), 1)
    lines = lax.broadcasted_iota(jnp.int32, (16, BLOCK), 0)

    def make_z(g):
        i = g if g < len(OWN) else FAR[g - len(OWN)]
        src = row if g < len(OWN) else y2 * 2 + c
        rows = GATHERS[g]
        half = rows // 2
        sector = src * 4 + OWN[i][0] // BLOCK
        for j in range(16):
            gate = jnp.concatenate([
                jnp.full((1, BLOCK), filled[sector, 2 * j + h].astype(jnp.float32)).astype(jnp.bfloat16)
                for h in range(2)], axis=1)
            psim[:half, j * COLS:(j + 1) * COLS] = bufs_a[g][j // 4, j % 4] * gate
            psim[half:rows, j * COLS:(j + 1) * COLS] = bufs_b[g][j % 4, j // 4] * gate
        ref = coded(src, i)

        def term(t, scales):
            value = jnp.dot(psim[:rows], right_v[t], preferred_element_type=jnp.float32)
            top = jnp.maximum(jnp.max(jnp.abs(value), axis=1, keepdims=True), 1e-30)
            level = jnp.ceil(jnp.log2(top) * 256.0 + 0.05)
            code = jnp.round(value * (jnp.exp2(level * (-1.0 / 256.0)) * TOP))
            ref[pl.ds(pl.multiple_of(t * rows, rows), rows), :] = code.astype(jnp.int32).astype(jnp.int16)
            line = jnp.sum(jnp.where(eye[:rows], level, 0.0), axis=0, keepdims=True)
            return jnp.where(lines == t, line, scales)

        scales = lax.fori_loop(0, TERMS, term, jnp.zeros((16, BLOCK), jnp.float32), unroll=True)
        ref[TERMS * rows:, :BLOCK] = scales.astype(jnp.int32).astype(jnp.int16)
        ref[TERMS * rows:, BLOCK:] = jnp.zeros((16, BLOCK), jnp.int16)

    def use_z(src, sector, pieces, rows):
        band = src * 4 + sector
        high, low, factors = [], [], []
        levels = [piece[TERMS * rows:, :BLOCK].astype(jnp.int32).astype(jnp.float32) for piece in pieces]
        for t in range(TERMS):
            for piece, level in zip(pieces, levels):
                scale = jnp.exp2(level[t:t + 1, :] * (1.0 / 256.0)) * (gates[t, band].astype(jnp.float32) / TOP)
                scale = jnp.sum(jnp.where(eye[:rows], scale, 0.0), axis=1, keepdims=True)
                value = piece[t * rows:(t + 1) * rows, :].astype(jnp.int32).astype(jnp.float32) * scale
                top = value.astype(jnp.bfloat16)
                high.append(top)
                low.append((value - top.astype(jnp.float32)).astype(jnp.bfloat16))
            factors.append(left_v[t, :, pl.ds(pl.multiple_of(band * BLOCK, BLOCK), BLOCK)])
        acc[...] += jnp.dot(jnp.concatenate(factors + factors, axis=1), jnp.concatenate(high + low, axis=0),
                            preferred_element_type=jnp.float32)

    plan = []
    todo = []

    def act(function, *args):
        todo.append((function, args))

    def make(g):
        act(wait_two, g)
        act(make_z, g)
        if g < len(OWN):
            for which in range(3):
                act(lambda which: z_copy(g, which).start(), which)
        else:
            act(lambda: z_copy(FAR[g - len(OWN)], 6).start())
        if g == 0:
            act(send_two, 3)
            act(loads[1].wait)
            for later in range(4, len(GATHERS)):
                act(send_one, later)
        elif 2 <= g < len(GATHERS) - 2:
            act(send_two, g + 2)

    def take(i, r):
        act(z_wait, i, r)
        if r == 2 and i not in FAR_OF:
            act(lambda: z_copy(i, 3).start())
        if r in (2, 3, 6):
            act(lambda: z_copy(i, {2: 4, 3: 5, 6: 6}[r]).start())

    for name, *args in ORDER:
        if name == "make":
            make(*args)
        elif name == "take":
            take(*args)
        else:
            sector, r = args
            for i in ((0, 1), (2,), (3,), (4,))[sector]:
                if r in (1, 4, 5, 7):
                    act(z_wait, i, r)
            plan.append((list(todo), sector, r))
            todo.clear()
    assert len(plan) == 32 and len({entry[1:] for entry in plan}) == 32 and not todo

    for g in range(len(OWN)):
        for copy in local(g):
            copy.wait()
    for g in range(3):
        send_one(g)
    for f in range(len(FAR)):
        for copy in far(f):
            copy.start()
    loads[0].start()
    loads[1].start()
    acc[...] = jnp.zeros_like(acc)
    send_two(0)
    send_two(1)
    send_one(3)
    send_two(2)
    loads[0].wait()

    def step(u, carry):
        sector, r = 0, 0
        for n, (actions, sector_n, r_n) in enumerate(plan):
            if actions:
                @pl.when(u == n)
                def _(actions=actions):
                    for function, args in actions:
                        function(*args)
            sector = jnp.where(u == n, sector_n, sector)
            r = jnp.where(u == n, r_n, r)
        y_of = jnp.where(r < 2, y, jnp.where(r >= 6, y2, jnp.where((r == 2) | (r == 5), yb, yf)))
        other = jnp.where((r == 1) | (r == 4) | (r == 5) | (r == 7), 1, 0)
        src = y_of * 2 + c + other * d

        @pl.when(sector == 0)
        def _():
            use_z(src, 0, [z_small.at[src, 0], z_small.at[src, 1]], 64)

        @pl.when(sector > 0)
        def _():
            use_z(src, sector, [z_large.at[src, sector - 1]], BLOCK)

        return carry

    lax.fori_loop(0, len(plan), step, 0)

    for i in range(4):
        for h in range(2):
            keep = filled[row * 4 + i, col * 2 + h].astype(jnp.float32)
            where = (slice(i * BLOCK, (i + 1) * BLOCK), slice(h * BLOCK, (h + 1) * BLOCK))
            out[where] = (acc[where] * keep).astype(jnp.bfloat16)

    for g in range(count):
        for slot in range(3):
            for copy in one(g, slot) + two(g, slot):
                copy.wait_send()
    for f in range(len(FAR)):
        for copy in far(f):
            copy.wait_send()
    for i in range(len(OWN)):
        for which in range(7):
            if which != 3 or i not in FAR_OF:
                z_copy(i, which).wait_send()


def on_device(wavefunction, left_env, right_env, filled_blocks, term_columns):
    any_space = pl.BlockSpec(memory_space=pl.ANY)
    smem = pl.BlockSpec(memory_space=pltpu.SMEM)
    dma = pltpu.SemaphoreType.DMA
    count = len(GATHERS)
    halves = [pltpu.VMEM((4, 4, rows // 2, COLS), jnp.bfloat16) for rows in GATHERS]
    return pl.pallas_call(
        kernel,
        out_shape=jax.ShapeDtypeStruct(wavefunction.shape, jnp.bfloat16),
        in_specs=[any_space, any_space, any_space, smem, smem],
        out_specs=pl.BlockSpec(memory_space=pltpu.VMEM),
        scratch_shapes=halves + halves + [
            pltpu.VMEM((BLOCK, DEEP), jnp.bfloat16),
            pltpu.VMEM((TERMS, DEEP, COLS), jnp.bfloat16),
            pltpu.VMEM((TERMS, 512, DEEP), jnp.bfloat16),
            pltpu.VMEM((8, 2, TERMS * 64 + 16, COLS), jnp.int16),
            pltpu.VMEM((8, 3, TERMS * BLOCK + 16, COLS), jnp.int16),
            pltpu.VMEM((512, COLS), jnp.float32),
            dma((count, 12)), dma((count, 12)), dma((2, 2)), dma((2, 2)),
            dma((len(OWN), 2)), dma((len(OWN), 7)), dma((len(OWN), 8)), dma((2,)),
        ],
        compiler_params=pltpu.CompilerParams(
            collective_id=0, has_side_effects=True, vmem_limit_bytes=60 * 1024 * 1024),
    )(wavefunction, left_env, right_env, filled_blocks, term_columns)


def solution(mesh):
    in_specs = (P("row", "col"), P(None, "row", None), P(None, None, "col"), P(), P())
    return jax.shard_map(on_device, mesh=mesh, in_specs=in_specs, out_specs=P("row", "col"), check_vma=False)
```

time: 192 us -> 65.4 us (0.34)
  waiting for transfers between devices: 145 us -> 0 us
  Pallas kernels: 0 us -> 63.6 us
  matrix products: 30.8 us -> 0 us
  between operations: 13.4 us -> 0.01 us
  other arithmetic: 2.47 us -> 0 us
    all_gather x2 -> x0, waiting for transfers between devices: 145 us -> none  [the longest x1 86 us: on_device(): lax.all_gather(right_terms, 'row', axis=1, tiled=True)]
    pallas_call x0 -> x1, Pallas kernels: none -> 63.6 us  [on_device(): pl.pallas_call(kernel, out_shape=jax.ShapeDtypeStruct(wavefunction.shape,...]
    dot_general x2 -> x0, matrix products: 30.8 us -> none  [the longest x1 20.3 us: on_device(): jnp.einsum('tak,tkb->ab', window, lax.all_gather(right_terms, 'row', axis...]
  transfers between devices with their start and end apart: 2 -> 0, of which waited for: 2 -> 0; matrix products, arithmetic and copies ran while one was open for 0% -> 0% of each run, Pallas kernels for 0% -> 0%
where the time goes in v3:
time: 65.4 us; the launch traced here: 65.2 us
  Pallas kernels  63.6 us (97%)
  local copies, waits for them, and re-layouts  1.67 us (3%)
    pallas_call x1, Pallas kernels, on_device(): pl.pallas_call(kernel, out_shape=jax.ShapeDtypeStruct(wavefunction.shape,...  63.6 us
    unnamed x1, local copies, waits for them, and re-layouts  1.67 us

profile of v3, /device:TPU:1, one launch (start us, length us, event | category | flops | bytes accessed | tf_op | source)
XLA Modules:
  0.0 65.2 jit_solution(3704692345459883344)
XLA Ops:
  0.0 63.6 %shard_map.55 = bf16[512,256]{1,0:T(8,128)(2,1)} custom-call(bf16[512,256]{1,0:T(8,128)(2,1)} %psi.1, bf16[4,512,4096]{2,1,0:T(8,128)(2,1)} %left.1, bf16[4,4096,256]{2,1,0:T(8,128)(2,1)} %right.1, s32[32,32]{1,0:T(8,128)} %filled.1, s32[4,32]{1,0:T(4,128)} %gates.1), custom_call_target="tpu_custom_call" | custom-call | tf_op jit(solution)/shard_map/pallas_call | solution.py:278
  63.6 1.7 %copy.7 = bf16[512,256]{1,0:T(8,128)(2,1)} copy(bf16[512,256]{1,0:T(8,128)(2,1)} %shard_map.55) | data formatting | bytes 524288

commit v4 on v3

--- a/solution.py
+++ b/solution.py
@@ -18,12 +18,12 @@
 GATHERS = [rows for _, rows in OWN] + [OWN[i][1] for i in FAR]
 FAR_OF = {i: len(OWN) + f for f, i in enumerate(FAR)}
 ORDER = (
-    ("make", 0), ("make", 1), ("use", 0, 0), ("make", 2), ("take", 0, 2), ("take", 0, 3), ("use", 0, 1),
-    ("use", 1, 0), ("take", 1, 2), ("take", 1, 3), ("use", 0, 2), ("use", 0, 3), ("use", 1, 1), ("make", 3),
-    ("use", 0, 4), ("use", 0, 5), ("use", 2, 0), ("use", 2, 1), ("take", 2, 2), ("take", 2, 3), ("use", 1, 2),
-    ("make", 4), ("take", 0, 6), ("take", 1, 6), ("use", 1, 3), ("use", 0, 6), ("use", 3, 0), ("use", 1, 4),
-    ("use", 1, 5), ("use", 0, 7), ("make", 5), ("take", 3, 2), ("take", 3, 3), ("use", 3, 1), ("use", 2, 2),
-    ("use", 2, 3), ("take", 2, 6), ("use", 3, 6), ("use", 1, 6), ("use", 2, 4), ("use", 2, 5), ("use", 3, 7),
+    ("make", 0), ("make", 1), ("use", 0, 0), ("use", 0, 1), ("make", 2), ("take", 0, 2), ("take", 0, 3),
+    ("use", 1, 0), ("take", 1, 2), ("take", 1, 3), ("use", 0, 2), ("use", 0, 3), ("use", 1, 1), ("use", 0, 4),
+    ("use", 0, 5), ("make", 3), ("use", 2, 0), ("use", 2, 1), ("take", 2, 2), ("take", 2, 3), ("use", 1, 2),
+    ("use", 1, 3), ("make", 4), ("take", 0, 6), ("take", 1, 6), ("use", 0, 6), ("use", 1, 4), ("use", 1, 5),
+    ("use", 3, 0), ("use", 3, 1), ("take", 3, 2), ("take", 3, 3), ("use", 0, 7), ("use", 2, 2), ("use", 2, 3),
+    ("make", 5), ("take", 2, 6), ("use", 1, 6), ("use", 3, 6), ("use", 2, 4), ("use", 2, 5), ("use", 3, 7),
     ("use", 1, 7), ("take", 4, 2), ("take", 4, 3), ("use", 3, 2), ("use", 3, 3), ("take", 3, 6), ("use", 2, 6),
     ("use", 3, 4), ("use", 3, 5), ("use", 2, 7),
 )
@@ -181,10 +181,12 @@
         if g == 0:
             act(send_two, 3)
             act(loads[1].wait)
-            for later in range(4, len(GATHERS)):
-                act(send_one, later)
-        elif 2 <= g < len(GATHERS) - 2:
-            act(send_two, g + 2)
+        if g == 1:
+            act(send_one, 5)
+        if g == 2:
+            act(send_two, 4)
+        if g == 3:
+            act(send_two, 5)
 
     def take(i, r):
         act(z_wait, i, r)
@@ -222,6 +224,7 @@
     send_two(1)
     send_one(3)
     send_two(2)
+    send_one(4)
     loads[0].wait()
 
     def step(u, carry):

time: 65.4 us -> 64.7 us (0.989)
  Pallas kernels: 63.6 us -> 62.8 us
    pallas_call x1, Pallas kernels: 63.6 us -> 62.8 us  [on_device(): pl.pallas_call(kernel, out_shape=jax.ShapeDtypeStruct(wavefunction.shape,...]
where the time goes in v4:
time: 64.7 us; the launch traced here: 64.5 us
  Pallas kernels  62.8 us (97%)
  local copies, waits for them, and re-layouts  1.67 us (3%)
    pallas_call x1, Pallas kernels, on_device(): pl.pallas_call(kernel, out_shape=jax.ShapeDtypeStruct(wavefunction.shape,...  62.8 us
    unnamed x1, local copies, waits for them, and re-layouts  1.67 us

profile of v4, /device:TPU:1, one launch (start us, length us, event | category | flops | bytes accessed | tf_op | source)
XLA Modules:
  0.0 64.5 jit_solution(6676337260186307242)
XLA Ops:
  0.0 62.8 %shard_map.55 = bf16[512,256]{1,0:T(8,128)(2,1)} custom-call(bf16[512,256]{1,0:T(8,128)(2,1)} %psi.1, bf16[4,512,4096]{2,1,0:T(8,128)(2,1)} %left.1, bf16[4,4096,256]{2,1,0:T(8,128)(2,1)} %right.1, s32[32,32]{1,0:T(8,128)} %filled.1, s32[4,32]{1,0:T(4,128)} %gates.1), custom_call_target="tpu_custom_call" | custom-call | tf_op jit(solution)/shard_map/pallas_call | solution.py:281
  62.8 1.7 %copy.7 = bf16[512,256]{1,0:T(8,128)(2,1)} copy(bf16[512,256]{1,0:T(8,128)(2,1)} %shard_map.55) | data formatting | bytes 524288

commit v5 on v4

--- a/solution.py
+++ b/solution.py
@@ -22,8 +22,8 @@
     ("use", 1, 0), ("take", 1, 2), ("take", 1, 3), ("use", 0, 2), ("use", 0, 3), ("use", 1, 1), ("use", 0, 4),
     ("use", 0, 5), ("make", 3), ("use", 2, 0), ("use", 2, 1), ("take", 2, 2), ("take", 2, 3), ("use", 1, 2),
     ("use", 1, 3), ("make", 4), ("take", 0, 6), ("take", 1, 6), ("use", 0, 6), ("use", 1, 4), ("use", 1, 5),
-    ("use", 3, 0), ("use", 3, 1), ("take", 3, 2), ("take", 3, 3), ("use", 0, 7), ("use", 2, 2), ("use", 2, 3),
-    ("make", 5), ("take", 2, 6), ("use", 1, 6), ("use", 3, 6), ("use", 2, 4), ("use", 2, 5), ("use", 3, 7),
+    ("use", 3, 0), ("use", 3, 1), ("take", 3, 2), ("take", 3, 3), ("make", 5), ("use", 0, 7), ("use", 2, 2),
+    ("use", 2, 3), ("take", 2, 6), ("use", 1, 6), ("use", 3, 6), ("use", 2, 4), ("use", 2, 5), ("use", 3, 7),
     ("use", 1, 7), ("take", 4, 2), ("take", 4, 3), ("use", 3, 2), ("use", 3, 3), ("take", 3, 6), ("use", 2, 6),
     ("use", 3, 4), ("use", 3, 5), ("use", 2, 7),
 )

time: 64.7 us -> 64.3 us (level)
  no operation moved by 1% of the time
where the time goes in v5:
time: 64.3 us; the launch traced here: 64.1 us
  Pallas kernels  62.5 us (97%)
  local copies, waits for them, and re-layouts  1.67 us (3%)
    pallas_call x1, Pallas kernels, on_device(): pl.pallas_call(kernel, out_shape=jax.ShapeDtypeStruct(wavefunction.shape,...  62.5 us
    unnamed x1, local copies, waits for them, and re-layouts  1.67 us

profile of v5, /device:TPU:1, one launch (start us, length us, event | category | flops | bytes accessed | tf_op | source)
XLA Modules:
  0.0 64.1 jit_solution(13718946216977308274)
XLA Ops:
  0.0 62.5 %shard_map.55 = bf16[512,256]{1,0:T(8,128)(2,1)} custom-call(bf16[512,256]{1,0:T(8,128)(2,1)} %psi.1, bf16[4,512,4096]{2,1,0:T(8,128)(2,1)} %left.1, bf16[4,4096,256]{2,1,0:T(8,128)(2,1)} %right.1, s32[32,32]{1,0:T(8,128)} %filled.1, s32[4,32]{1,0:T(4,128)} %gates.1), custom_call_target="tpu_custom_call" | custom-call | tf_op jit(solution)/shard_map/pallas_call | solution.py:281
  62.5 1.7 %copy.7 = bf16[512,256]{1,0:T(8,128)(2,1)} copy(bf16[512,256]{1,0:T(8,128)(2,1)} %shard_map.55) | data formatting | bytes 524288
